TPU v7x, 32 devices: a whole 2x2x4 slice. The times are simulated.
32 devices in a mesh: rep: 4 (over y, core), shard: 8 (over z, x).
Axes of the slice: x: 2, y: 2, z: 4, core: 2. Of those that a mesh axis runs over, the one named last changes fastest.
Arguments:
- layer_input: bfloat16 [32, 197, 768], P(('rep', 'shard')), may hold values from -6 to 6
- cotangent: bfloat16 [32, 197, 768], P(('rep', 'shard')), may hold values from -6 to 6
- live: int32 [32], P(('rep', 'shard')), may hold values 0 or 1
- first_gain: bfloat16 [768], P('shard'), may hold values from 0.099609375 to 1.8984375
- first_bias: bfloat16 [768], P('shard'), may hold values from -3 to 3
- qkv_weight: bfloat16 [768, 2304], P('shard'), may hold values from -0.21875 to 0.21875
- query_bias: bfloat16 [768], P('shard'), may hold values from -3 to 3
- value_bias: bfloat16 [768], P('shard'), may hold values from -3 to 3
- out_weight: bfloat16 [768, 768], P('shard'), may hold values from -1.5 to 1.5
- out_bias: bfloat16 [768], P('shard'), may hold values from -3 to 3
- second_gain: bfloat16 [768], P('shard'), may hold values from 0.099609375 to 1.8984375
- second_bias: bfloat16 [768], P('shard'), may hold values from -3 to 3
- up_weight: bfloat16 [768, 3072], P('shard'), may hold values from -0.21875 to 0.21875
- up_bias: bfloat16 [3072], P('shard'), may hold values from -3 to 3
- down_weight: bfloat16 [3072, 768], P('shard'), may hold values from -0.109375 to 0.109375
- down_bias: bfloat16 [768], P('shard'), may hold values from -3 to 3
Outputs:
- output: bfloat16 [32, 197, 768], P(('rep', 'shard'))
- input_grad: bfloat16 [32, 197, 768], P(('rep', 'shard'))
- first_gain_grad: float32 [768], P('shard')
- first_bias_grad: float32 [768], P('shard')
- qkv_weight_grad: float32 [768, 2304], P('shard')
- query_bias_grad: float32 [768], P('shard')
- value_bias_grad: float32 [768], P('shard')
- out_weight_grad: float32 [768, 768], P('shard')
- out_bias_grad: float32 [768], P('shard')
- second_gain_grad: float32 [768], P('shard')
- second_bias_grad: float32 [768], P('shard')
- up_weight_grad: float32 [768, 3072], P('shard')
- up_bias_grad: float32 [3072], P('shard')
- down_weight_grad: float32 [3072, 768], P('shard')
- down_bias_grad: float32 [768], P('shard')
All inputs are finite; a program needn't handle non-finite values. No bound on the sum of `live` on one device may be relied on, other than what follows from the above.
Results may differ from a plain program's by a relative error of at most 0.014.
Values may be sent and summed in bfloat16 or wider, within the bound.
A program may use at most 128 MiB of HBM per device.

v0:
```python
import jax
import jax.numpy as jnp
from jax import lax
from jax.sharding import PartitionSpec as P

HEAD_DIM = 64
norm_eps = 1e-06
root_half = 0.7071067811865476
density_coef = 0.3989422804014327


def matmul(operand, factor):
    flat = operand.reshape(-1, operand.shape[-1])
    product = jnp.dot(flat, factor, preferred_element_type=jnp.float32)
    return product.reshape(operand.shape[:-1] + (factor.shape[-1],))


def outer_product(operand, factor):
    return jnp.dot(
        operand.reshape(-1, operand.shape[-1]).T,
        factor.reshape(-1, factor.shape[-1]),
        preferred_element_type=jnp.float32,
    )


def batched(form, operand, factor):
    return jnp.einsum(form, operand, factor, preferred_element_type=jnp.float32)


def layer_norm(values, norm_gain, norm_bias):
    average = jnp.mean(values, axis=-1, keepdims=True)
    centred = values - average
    spread = jnp.mean(centred * centred, axis=-1, keepdims=True)
    inv_std = lax.rsqrt(spread + norm_eps)
    hat_vals = centred * inv_std
    return (
        hat_vals * norm_gain.astype(jnp.float32) + norm_bias.astype(jnp.float32),
        hat_vals,
        inv_std,
    )


def norm_back(incoming, hat_vals, inv_std, norm_gain):
    scaled = incoming * norm_gain.astype(jnp.float32)
    return inv_std * (
        scaled
        - jnp.mean(scaled, axis=-1, keepdims=True)
        - hat_vals * jnp.mean(scaled * hat_vals, axis=-1, keepdims=True)
    )


def forward_pass(params, layer_input, live):
    (
        first_gain,
        first_bias,
        qkv_weight,
        query_bias,
        value_bias,
        out_weight,
        out_bias,
        second_gain,
        second_bias,
        up_weight,
        up_bias,
        down_weight,
        down_bias,
    ) = params
    images, length, model_width = layer_input.shape
    head_count = model_width // HEAD_DIM
    score_scale = HEAD_DIM ** (-0.5)
    stream = layer_input.astype(jnp.float32)
    normed, first_hat, first_inv = layer_norm(stream, first_gain, first_bias)
    normed = normed.astype(jnp.bfloat16)
    projected = matmul(normed, qkv_weight)
    shape_heads = (images, length, head_count, HEAD_DIM)
    queries = (
        (projected[..., :model_width] + query_bias.astype(jnp.float32))
        .astype(jnp.bfloat16)
        .reshape(shape_heads)
    )
    key_rows = (
        projected[..., model_width : 2 * model_width].astype(jnp.bfloat16).reshape(shape_heads)
    )
    values = (
        (projected[..., 2 * model_width :] + value_bias.astype(jnp.float32))
        .astype(jnp.bfloat16)
        .reshape(shape_heads)
    )
    scores = batched("bqhd,bkhd->bhqk", queries, key_rows) * score_scale
    log_total = jnp.log(jnp.sum(jnp.exp(scores), axis=-1, keepdims=True))
    weights = jnp.exp(scores - log_total).astype(jnp.bfloat16)
    attended = (
        batched("bhqk,bkhd->bqhd", weights, values)
        .reshape(images, length, model_width)
        .astype(jnp.bfloat16)
    )
    middle = stream + matmul(attended, out_weight) + out_bias.astype(jnp.float32)
    second_normed, second_hat, second_inv = layer_norm(middle, second_gain, second_bias)
    second_normed = second_normed.astype(jnp.bfloat16)
    hidden_pre = matmul(second_normed, up_weight) + up_bias.astype(jnp.float32)
    normal_cdf = 0.5 * (1.0 + lax.erf(hidden_pre * root_half))
    hidden = (hidden_pre * normal_cdf).astype(jnp.bfloat16)
    result = middle + matmul(hidden, down_weight) + down_bias.astype(jnp.float32)
    image_mask = live.astype(jnp.float32)[:, None, None]
    output = (result * image_mask).astype(jnp.bfloat16)
    saved = (
        normed,
        first_hat,
        first_inv,
        queries,
        key_rows,
        values,
        log_total,
        attended,
        second_normed,
        second_hat,
        second_inv,
        hidden_pre,
        normal_cdf,
        hidden,
        image_mask,
    )
    return (output, saved)


def backward_pass(params, saved, cotangent):
    (
        first_gain,
        first_bias,
        qkv_weight,
        query_bias,
        value_bias,
        out_weight,
        out_bias,
        second_gain,
        second_bias,
        up_weight,
        up_bias,
        down_weight,
        down_bias,
    ) = params
    (
        normed,
        first_hat,
        first_inv,
        queries,
        key_rows,
        values,
        log_total,
        attended,
        second_normed,
        second_hat,
        second_inv,
        hidden_pre,
        normal_cdf,
        hidden,
        image_mask,
    ) = saved
    images, length, head_count, head_width = queries.shape
    flat_shape = (images, length, head_count * head_width)
    score_scale = HEAD_DIM ** (-0.5)
    upstream = cotangent.astype(jnp.float32) * image_mask
    upstream_low = upstream.astype(jnp.bfloat16)
    down_weight_grad = outer_product(hidden, upstream_low)
    down_bias_grad = jnp.sum(upstream, axis=(0, 1))
    hidden_grad = matmul(upstream_low, down_weight.T)
    density = jnp.exp(-0.5 * hidden_pre * hidden_pre) * density_coef
    pre_grad = hidden_grad * (normal_cdf + hidden_pre * density)
    pre_low = pre_grad.astype(jnp.bfloat16)
    up_weight_grad = outer_product(second_normed, pre_low)
    up_bias_grad = jnp.sum(pre_grad, axis=(0, 1))
    second_in = matmul(pre_low, up_weight.T)
    second_gain_grad = jnp.sum(second_in * second_hat, axis=(0, 1))
    second_bias_grad = jnp.sum(second_in, axis=(0, 1))
    middle_grad = upstream + norm_back(second_in, second_hat, second_inv, second_gain)
    middle_low = middle_grad.astype(jnp.bfloat16)
    out_weight_grad = outer_product(attended, middle_low)
    out_bias_grad = jnp.sum(middle_grad, axis=(0, 1))
    attended_grad = matmul(middle_low, out_weight.T).astype(jnp.bfloat16).reshape(queries.shape)
    again_scores = batched("bqhd,bkhd->bhqk", queries, key_rows) * score_scale
    probs = jnp.exp(again_scores - log_total)
    probs_low = probs.astype(jnp.bfloat16)
    value_grad = batched("bhqk,bqhd->bkhd", probs_low, attended_grad)
    prob_grad = batched("bqhd,bkhd->bhqk", attended_grad, values)
    score_grad = (
        probs * (prob_grad - jnp.sum(probs * prob_grad, axis=-1, keepdims=True)) * score_scale
    ).astype(jnp.bfloat16)
    query_grad = batched("bhqk,bkhd->bqhd", score_grad, key_rows).reshape(flat_shape)
    key_grad = batched("bhqk,bqhd->bkhd", score_grad, queries).reshape(flat_shape)
    value_grad = value_grad.reshape(flat_shape)
    joined = jnp.concatenate([query_grad, key_grad, value_grad], axis=-1).astype(jnp.bfloat16)
    qkv_weight_grad = outer_product(normed, joined)
    query_bias_grad = jnp.sum(query_grad, axis=(0, 1))
    value_bias_grad = jnp.sum(value_grad, axis=(0, 1))
    first_in = matmul(joined, qkv_weight.T)
    first_gain_grad = jnp.sum(first_in * first_hat, axis=(0, 1))
    first_bias_grad = jnp.sum(first_in, axis=(0, 1))
    middle_grad = middle_grad + norm_back(first_in, first_hat, first_inv, first_gain)
    input_grad = middle_grad.astype(jnp.bfloat16)
    grads = (
        first_gain_grad,
        first_bias_grad,
        qkv_weight_grad,
        query_bias_grad,
        value_bias_grad,
        out_weight_grad,
        out_bias_grad,
        second_gain_grad,
        second_bias_grad,
        up_weight_grad,
        up_bias_grad,
        down_weight_grad,
        down_bias_grad,
    )
    return (input_grad, grads)


def per_device(
    layer_input,
    cotangent,
    live,
    first_gain,
    first_bias,
    qkv_weight,
    query_bias,
    value_bias,
    out_weight,
    out_bias,
    second_gain,
    second_bias,
    up_weight,
    up_bias,
    down_weight,
    down_bias,
):
    gathered = (
        lax.all_gather(first_gain, "shard", axis=0, tiled=True),
        lax.all_gather(first_bias, "shard", axis=0, tiled=True),
        lax.all_gather(qkv_weight, "shard", axis=0, tiled=True),
        lax.all_gather(query_bias, "shard", axis=0, tiled=True),
        lax.all_gather(value_bias, "shard", axis=0, tiled=True),
        lax.all_gather(out_weight, "shard", axis=0, tiled=True),
        lax.all_gather(out_bias, "shard", axis=0, tiled=True),
        lax.all_gather(second_gain, "shard", axis=0, tiled=True),
        lax.all_gather(second_bias, "shard", axis=0, tiled=True),
        lax.all_gather(up_weight, "shard", axis=0, tiled=True),
        lax.all_gather(up_bias, "shard", axis=0, tiled=True),
        lax.all_gather(down_weight, "shard", axis=0, tiled=True),
        lax.all_gather(down_bias, "shard", axis=0, tiled=True),
    )
    output, saved = forward_pass(gathered, layer_input, live)
    backward_params = (
        lax.all_gather(first_gain, "shard", axis=0, tiled=True),
        lax.all_gather(first_bias, "shard", axis=0, tiled=True),
        lax.all_gather(qkv_weight, "shard", axis=0, tiled=True),
        lax.all_gather(query_bias, "shard", axis=0, tiled=True),
        lax.all_gather(value_bias, "shard", axis=0, tiled=True),
        lax.all_gather(out_weight, "shard", axis=0, tiled=True),
        lax.all_gather(out_bias, "shard", axis=0, tiled=True),
        lax.all_gather(second_gain, "shard", axis=0, tiled=True),
        lax.all_gather(second_bias, "shard", axis=0, tiled=True),
        lax.all_gather(up_weight, "shard", axis=0, tiled=True),
        lax.all_gather(up_bias, "shard", axis=0, tiled=True),
        lax.all_gather(down_weight, "shard", axis=0, tiled=True),
        lax.all_gather(down_bias, "shard", axis=0, tiled=True),
    )
    input_grad, grads = backward_pass(backward_params, saved, cotangent)
    g00, g01, g02, g03, g04, g05, g06, g07, g08, g09, g10, g11, g12 = grads
    owned = (
        lax.psum_scatter(g00, "shard", scatter_dimension=0, tiled=True),
        lax.psum_scatter(g01, "shard", scatter_dimension=0, tiled=True),
        lax.psum_scatter(g02, "shard", scatter_dimension=0, tiled=True),
        lax.psum_scatter(g03, "shard", scatter_dimension=0, tiled=True),
        lax.psum_scatter(g04, "shard", scatter_dimension=0, tiled=True),
        lax.psum_scatter(g05, "shard", scatter_dimension=0, tiled=True),
        lax.psum_scatter(g06, "shard", scatter_dimension=0, tiled=True),
        lax.psum_scatter(g07, "shard", scatter_dimension=0, tiled=True),
        lax.psum_scatter(g08, "shard", scatter_dimension=0, tiled=True),
        lax.psum_scatter(g09, "shard", scatter_dimension=0, tiled=True),
        lax.psum_scatter(g10, "shard", scatter_dimension=0, tiled=True),
        lax.psum_scatter(g11, "shard", scatter_dimension=0, tiled=True),
        lax.psum_scatter(g12, "shard", scatter_dimension=0, tiled=True),
    )
    o00, o01, o02, o03, o04, o05, o06, o07, o08, o09, o10, o11, o12 = owned
    quarter = (
        lax.psum_scatter(o00.astype(jnp.bfloat16), "rep", scatter_dimension=0, tiled=True).astype(
            jnp.float32
        ),
        lax.psum_scatter(o01.astype(jnp.bfloat16), "rep", scatter_dimension=0, tiled=True).astype(
            jnp.float32
        ),
        lax.psum_scatter(o02.astype(jnp.bfloat16), "rep", scatter_dimension=0, tiled=True).astype(
            jnp.float32
        ),
        lax.psum_scatter(o03.astype(jnp.bfloat16), "rep", scatter_dimension=0, tiled=True).astype(
            jnp.float32
        ),
        lax.psum_scatter(o04.astype(jnp.bfloat16), "rep", scatter_dimension=0, tiled=True).astype(
            jnp.float32
        ),
        lax.psum_scatter(o05.astype(jnp.bfloat16), "rep", scatter_dimension=0, tiled=True).astype(
            jnp.float32
        ),
        lax.psum_scatter(o06.astype(jnp.bfloat16), "rep", scatter_dimension=0, tiled=True).astype(
            jnp.float32
        ),
        lax.psum_scatter(o07.astype(jnp.bfloat16), "rep", scatter_dimension=0, tiled=True).astype(
            jnp.float32
        ),
        lax.psum_scatter(o08.astype(jnp.bfloat16), "rep", scatter_dimension=0, tiled=True).astype(
            jnp.float32
        ),
        lax.psum_scatter(o09.astype(jnp.bfloat16), "rep", scatter_dimension=0, tiled=True).astype(
            jnp.float32
        ),
        lax.psum_scatter(o10.astype(jnp.bfloat16), "rep", scatter_dimension=0, tiled=True).astype(
            jnp.float32
        ),
        lax.psum_scatter(o11.astype(jnp.bfloat16), "rep", scatter_dimension=0, tiled=True).astype(
            jnp.float32
        ),
        lax.psum_scatter(o12.astype(jnp.bfloat16), "rep", scatter_dimension=0, tiled=True).astype(
            jnp.float32
        ),
    )
    q00, q01, q02, q03, q04, q05, q06, q07, q08, q09, q10, q11, q12 = quarter
    summed = (
        lax.all_gather(q00.astype(jnp.bfloat16), "rep", axis=0, tiled=True).astype(q00.dtype),
        lax.all_gather(q01.astype(jnp.bfloat16), "rep", axis=0, tiled=True).astype(q01.dtype),
        lax.all_gather(q02.astype(jnp.bfloat16), "rep", axis=0, tiled=True).astype(q02.dtype),
        lax.all_gather(q03.astype(jnp.bfloat16), "rep", axis=0, tiled=True).astype(q03.dtype),
        lax.all_gather(q04.astype(jnp.bfloat16), "rep", axis=0, tiled=True).astype(q04.dtype),
        lax.all_gather(q05.astype(jnp.bfloat16), "rep", axis=0, tiled=True).astype(q05.dtype),
        lax.all_gather(q06.astype(jnp.bfloat16), "rep", axis=0, tiled=True).astype(q06.dtype),
        lax.all_gather(q07.astype(jnp.bfloat16), "rep", axis=0, tiled=True).astype(q07.dtype),
        lax.all_gather(q08.astype(jnp.bfloat16), "rep", axis=0, tiled=True).astype(q08.dtype),
        lax.all_gather(q09.astype(jnp.bfloat16), "rep", axis=0, tiled=True).astype(q09.dtype),
        lax.all_gather(q10.astype(jnp.bfloat16), "rep", axis=0, tiled=True).astype(q10.dtype),
        lax.all_gather(q11.astype(jnp.bfloat16), "rep", axis=0, tiled=True).astype(q11.dtype),
        lax.all_gather(q12.astype(jnp.bfloat16), "rep", axis=0, tiled=True).astype(q12.dtype),
    )
    return (
        output,
        input_grad,
        summed[0],
        summed[1],
        summed[2],
        summed[3],
        summed[4],
        summed[5],
        summed[6],
        summed[7],
        summed[8],
        summed[9],
        summed[10],
        summed[11],
        summed[12],
    )


def solution(mesh):
    placed = (
        P(("rep", "shard"), None, None),
        P(("rep", "shard"), None, None),
        P(("rep", "shard")),
        P("shard"),
        P("shard"),
        P("shard", None),
        P("shard"),
        P("shard"),
        P("shard", None),
        P("shard"),
        P("shard"),
        P("shard"),
        P("shard", None),
        P("shard"),
        P("shard", None),
        P("shard"),
    )
    return jax.shard_map(
        per_device,
        mesh=mesh,
        in_specs=placed,
        out_specs=(
            P(("rep", "shard"), None, None),
            P(("rep", "shard"), None, None),
            P("shard"),
            P("shard"),
            P("shard", None),
            P("shard"),
            P("shard"),
            P("shard", None),
            P("shard"),
            P("shard"),
            P("shard"),
            P("shard", None),
            P("shard"),
            P("shard", None),
            P("shard"),
        ),
        check_vma=False,
    )
```

profile of v0, /device:TPU:0, one launch (start us, length us, event | category | flops | bytes accessed | tf_op | source)
XLA Modules:
  0.0 931.1 jit_solution(7860005917995283044)
XLA Ops:
  18.7 40.4 %all-reduce.36 = (bf16[768]{0:T(1024)(128)(2,1)S(1)}, bf16[768]{0:T(1024)(128)(2,1)S(1)}, bf16[768]{0:T(1024)(128)(2,1)S(1)}, bf16[768]{0:T(1024)(128)(2,1)S(1)}...) all-reduce(bf16[768]{0:T(1024)(128)(2,1)S(1)} %dynamic-update-slice, ...), channel_id=1, replica_groups=mesh['rep'=4,'shard'=8] {'shard'}, use_global_device_ids=true, to_apply=%add.1 | all-reduce | flops 6144 | bytes 24576
  60.5 26.5 %all-gather = bf16[8,1,384]{2,1,0:T(2,128)(2,1)S(1)} all-gather(bf16[1,1,384]{2,1,0:T(2,128)(2,1)S(1)} %reshape.374), channel_id=1, replica_groups=mesh['rep'=4,'shard'=8] {'shard'}, dimensions={0}, use_global_device_ids=true | all-gather | bytes 6912 | tf_op jit(solution)/shard_map/all_gather | solution.py:247
  99.2 21.3 %all-gather.8.cloned.1.call-done = bf16[768,768]{1,0:T(8,128)(2,1)} async-done(((bf16[96,768]{1,0:T(8,128)(2,1)}), bf16[768,768]{1,0:T(8,128)(2,1)}) %all-gather.8.cloned.1.call-update) | async-done | bytes 1179664 | tf_op jit(solution)/shard_map/all_gather | solution.py:242
  122.5 78.2 %all-gather.10.cloned.1.call-done = bf16[768,3072]{1,0:T(8,128)(2,1)} async-done(((bf16[96,3072]{1,0:T(8,128)(2,1)}), bf16[768,3072]{1,0:T(8,128)(2,1)}) %all-gather.10.cloned.1.call-update) | async-done | bytes 4718608 | tf_op jit(solution)/shard_map/all_gather | solution.py:246
  204.3 76.2 %all-gather.12.cloned.1.call-done = bf16[3072,768]{1,0:T(8,128)(2,1)} async-done(((bf16[384,768]{1,0:T(8,128)(2,1)}), bf16[3072,768]{1,0:T(8,128)(2,1)}) %all-gather.12.cloned.1.call-update) | async-done | bytes 4718608 | tf_op jit(solution)/shard_map/all_gather | solution.py:248
  306.1 5.6 fusion.23
  311.7 5.5 fusion.109
  322.7 6.5 fusion.56
  329.3 5.6 fusion.80
  335.0 23.1 %reduce-scatter.13.cloned.1.call-done = f32[96,768]{1,0:T(8,128)} async-done(((f32[768,768]{1,0:T(8,128)}), f32[96,768]{1,0:T(8,128)}) %reduce-scatter.13.cloned.1.call-update) | async-done | bytes 294928 | tf_op jit(solution)/shard_map/reduce_scatter | solution.py:275
  359.8 130.2 %reduce-scatter.9.cloned.1.call-done = f32[96,2304]{1,0:T(8,128)} async-done(((f32[768,2304]{1,0:T(8,128)}), f32[96,2304]{1,0:T(8,128)}) %reduce-scatter.9.cloned.1.call-update) | async-done | bytes 884752 | tf_op jit(solution)/shard_map/reduce_scatter | solution.py:272
  492.1 162.8 %reduce-scatter.17.cloned.1.call-done = f32[96,3072]{1,0:T(8,128)} async-done(((f32[768,3072]{1,0:T(8,128)}), f32[96,3072]{1,0:T(8,128)}) %reduce-scatter.17.cloned.1.call-update) | async-done | bytes 1179664 | tf_op jit(solution)/shard_map/reduce_scatter | solution.py:279
  666.0 38.6 %all-reduce.35 = (bf16[768]{0:T(1024)(128)(2,1)S(1)}, bf16[768]{0:T(1024)(128)(2,1)S(1)}, bf16[768]{0:T(1024)(128)(2,1)S(1)}, bf16[768]{0:T(1024)(128)(2,1)S(1)}...) all-reduce(f32[768]{0:T(1024)S(1)} %get-tuple-element.17, ...), channel_id=2, replica_groups=mesh['rep'=4,'shard'=8] {'shard'}, use_global_device_ids=true, to_apply=%region_11.0.clone | all-reduce | flops 9216 | bytes 55296
  705.3 6.4 all-reduce.38
  714.2 6.7 all-reduce.37
  725.6 95.5 %reduce-scatter.21.cloned.1.call-done = f32[384,768]{1,0:T(8,128)} async-done(((f32[3072,768]{1,0:T(8,128)}), f32[384,768]{1,0:T(8,128)}) %reduce-scatter.21.cloned.1.call-update) | async-done | bytes 1179664 | tf_op jit(solution)/shard_map/reduce_scatter | solution.py:281
  829.9 13.0 %reduce-scatter.15.cloned.1.call-done = bf16[24,768]{1,0:T(8,128)(2,1)} async-done(((bf16[96,768]{1,0:T(8,128)(2,1)}), bf16[24,768]{1,0:T(8,128)(2,1)}) %reduce-scatter.15.cloned.1.call-update) | async-done | bytes 36880 | tf_op jit(solution)/shard_map/reduce_scatter | solution.py:301
  842.9 5.7 all_gather.102
  849.3 17.1 %reduce-scatter.11.cloned.1.call-done = bf16[24,2304]{1,0:T(8,128)(2,1)} async-done(((bf16[96,2304]{1,0:T(8,128)(2,1)}), bf16[24,2304]{1,0:T(8,128)(2,1)}) %reduce-scatter.11.cloned.1.call-update) | async-done | bytes 110608 | tf_op jit(solution)/shard_map/reduce_scatter | solution.py:292
  866.3 6.5 all_gather.99
  873.8 17.8 %reduce-scatter.19.cloned.1.call-done = bf16[24,3072]{1,0:T(8,128)(2,1)} async-done(((bf16[96,3072]{1,0:T(8,128)(2,1)}), bf16[24,3072]{1,0:T(8,128)(2,1)}) %reduce-scatter.19.cloned.1.call-update) | async-done | bytes 147472 | tf_op jit(solution)/shard_map/reduce_scatter | solution.py:313
  891.5 7.1 all_gather.106
  899.8 16.2 %reduce-scatter.23.cloned.1.call-done = bf16[96,768]{1,0:T(8,128)(2,1)} async-done(((bf16[384,768]{1,0:T(8,128)(2,1)}), bf16[96,768]{1,0:T(8,128)(2,1)}) %reduce-scatter.23.cloned.1.call-update) | async-done | bytes 147472 | tf_op jit(solution)/shard_map/reduce_scatter | solution.py:319
  916.0 7.1 all_gather.108
  (163 shorter events, 92.0 us)
Async XLA Ops:
  7.2 80.9 %copy-start = (bf16[1,197,768]{2,1,0:T(8,128)(2,1)S(1)}, bf16[1,197,768]{2,1,0:T(8,128)(2,1)}, u32[]{:S(2)}) copy-start(bf16[1,197,768]{2,1,0:T(8,128)(2,1)} %param.16) | copy-start | bytes 907780
  7.2 81.2 %all-gather.6.cloned.1.call-start = ((), (), s32[]{:S(2)}) async-start(), calls=%async_computation.8 | async-start | bytes 3981312 | tf_op jit(solution)/shard_map/all_gather | solution.py:239
  7.9 112.5 %all-gather.8.cloned.1.call-start = ((), (), s32[]{:S(2)}) async-start(), calls=%async_computation.9 | async-start | bytes 1327104 | tf_op jit(solution)/shard_map/all_gather | solution.py:242
  8.7 192.0 %all-gather.10.cloned.1.call-start = ((), (), s32[]{:S(2)}) async-start(), calls=%async_computation.10 | async-start | bytes 5308416 | tf_op jit(solution)/shard_map/all_gather | solution.py:246
  9.4 271.1 %all-gather.12.cloned.1.call-start = ((), (), s32[]{:S(2)}) async-start(), calls=%async_computation.11 | async-start | bytes 5308416 | tf_op jit(solution)/shard_map/all_gather | solution.py:248
  10.0 348.1 %reduce-scatter.13.cloned.1.call-start = ((), (), s32[]{:S(2)}) async-start(), calls=%async_computation.14 | async-start | bytes 2654208 | tf_op jit(solution)/shard_map/reduce_scatter | solution.py:275
  95.2 1.7 copy-start.7
  96.9 23.6 %copy-start.4 = (f32[12,197,197]{1,2,0:T(8,128)}, f32[12,197,197]{1,2,0:T(8,128)S(1)}, u32[]{:S(2)}) copy-start(f32[12,197,197]{1,2,0:T(8,128)S(1)} %fusion.118) | copy-start | bytes 5588500
  99.2 101.5 %copy-start.5 = (bf16[12,64,197]{2,1,0:T(8,128)(2,1)}, bf16[12,64,197]{2,1,0:T(8,128)(2,1)S(1)}, u32[]{:S(2)}) copy-start(bf16[12,64,197]{2,1,0:T(8,128)(2,1)S(1)} %convolution_convert_fusion) | copy-start | bytes 907780
  280.5 4.4 copy-start.2
  284.8 1.8 copy-start.9
  284.8 2.0 copy-start.8
  286.7 1.4 copy-start.6
  287.2 0.8 copy-start.1
  289.9 200.1 %reduce-scatter.9.cloned.1.call-start = ((), (), s32[]{:S(2)}) async-start(), calls=%async_computation.12 | async-start | bytes 7962624 | tf_op jit(solution)/shard_map/reduce_scatter | solution.py:272
  322.7 332.2 %reduce-scatter.17.cloned.1.call-start = ((), (), s32[]{:S(2)}) async-start(), calls=%async_computation.16 | async-start | bytes 10616832 | tf_op jit(solution)/shard_map/reduce_scatter | solution.py:279
  329.3 491.8 %reduce-scatter.21.cloned.1.call-start = ((), (), s32[]{:S(2)}) async-start(), calls=%async_computation.18 | async-start | bytes 10616832 | tf_op jit(solution)/shard_map/reduce_scatter | solution.py:281
  334.9 507.9 %reduce-scatter.15.cloned.1.call-start = ((), (), s32[]{:S(2)}) async-start(), calls=%async_computation.15 | async-start | bytes 184320 | tf_op jit(solution)/shard_map/reduce_scatter | solution.py:301
  359.8 506.6 %reduce-scatter.11.cloned.1.call-start = ((), (), s32[]{:S(2)}) async-start(), calls=%async_computation.13 | async-start | bytes 552960 | tf_op jit(solution)/shard_map/reduce_scatter | solution.py:292
  492.0 399.5 %reduce-scatter.19.cloned.1.call-start = ((), (), s32[]{:S(2)}) async-start(), calls=%async_computation.17 | async-start | bytes 737280 | tf_op jit(solution)/shard_map/reduce_scatter | solution.py:313
  657.1 258.9 %reduce-scatter.23.cloned.1.call-start = ((), (), s32[]{:S(2)}) async-start(), calls=%async_computation.19 | async-start | bytes 737280 | tf_op jit(solution)/shard_map/reduce_scatter | solution.py:319
  665.0 0.8 copy-start.3
Sparse Core Ops, SparseCore 0:
  10.2 68.0 all-gather.5
  80.4 39.9 all-gather.7
  122.7 78.0 all-gather.9
  202.7 77.6 all-gather.11
  290.0 68.0 reduce-scatter.12
  361.6 128.3 reduce-scatter.8
  493.6 161.2 reduce-scatter.16
  658.5 162.5 reduce-scatter.20
  824.1 18.7 reduce-scatter.14
  845.2 21.0 reduce-scatter.10
  869.4 22.0 reduce-scatter.18
  893.9 22.0 reduce-scatter.22
where the time goes:
time: 932 us; the launch traced here: 931 us
  waiting for transfers between devices  654 us (70%)
  blocking collectives  145 us (16%)
  matrix products  71.3 us (8%)
  other arithmetic  21.1 us (2%)
  between operations  19.7 us (2%)
  local copies, waits for them, and re-layouts  19.4 us (2%)
    reduce_scatter x1, waiting for transfers between devices, per_device(): lax.psum_scatter(g09, 'shard', scatter_dimension=0, tiled=True)  163 us
    reduce_scatter x1, waiting for transfers between devices, per_device(): lax.psum_scatter(g02, 'shard', scatter_dimension=0, tiled=True)  130 us
    reduce_scatter x1, waiting for transfers between devices, per_device(): lax.psum_scatter(g11, 'shard', scatter_dimension=0, tiled=True)  95.5 us
    unnamed x4, blocking collectives  92 us
    all_gather x1, waiting for transfers between devices, per_device(): lax.all_gather(up_weight, 'shard', axis=0, tiled=True)  78.2 us
    all_gather x1, waiting for transfers between devices, per_device(): lax.all_gather(down_weight, 'shard', axis=0, tiled=True)  76.2 us
    all_gather x1, blocking collectives, per_device(): lax.all_gather(up_bias, 'shard', axis=0, tiled=True)  26.5 us
    dot_general x8, matrix products, matmul(): product = jnp.dot(flat, factor, preferred_element_type=jnp.float32)  25.5 us
  transfers between devices with their start and end apart: 12, of which 11 were waited for; matrix products, arithmetic and copies ran while one was open for 11% of the time, Pallas kernels for 0%

commit v1 on v0

--- a/solution.py
+++ b/solution.py
@@ -245,7 +245,12 @@
         lax.all_gather(second_bias, "shard", axis=0, tiled=True),
         lax.all_gather(up_weight, "shard", axis=0, tiled=True),
         lax.all_gather(up_bias, "shard", axis=0, tiled=True),
-        lax.all_gather(down_weight, "shard", axis=0, tiled=True),
+        jnp.concatenate(
+            lax.all_to_all(
+                jnp.stack([down_weight for _ in range(lax.psum(1, "shard"))], 0), "shard", 0, 0
+            ),
+            0,
+        ),
         lax.all_gather(down_bias, "shard", axis=0, tiled=True),
     )
     output, saved = forward_pass(gathered, layer_input, live)

time: 932 us -> 1020 us (1.094)
  waiting for transfers between devices: 654 us -> 733 us
    reduce_scatter x1, waiting for transfers between devices: 130 us -> 191 us  [per_device(): lax.psum_scatter(g02, 'shard', scatter_dimension=0, tiled=True)]
    reduce_scatter x1, waiting for transfers between devices: 23.1 us -> 41.4 us  [per_device(): lax.psum_scatter(g05, 'shard', scatter_dimension=0, tiled=True)]
  transfers between devices with their start and end apart: 12 -> 13, of which waited for: 11 -> 11; matrix products, arithmetic and copies ran while one was open for 11% -> 10% of each run, Pallas kernels for 0% -> 0%
where the time goes in v1:
time: 1020 us
  waiting for transfers between devices  733 us (72%)
  blocking collectives  145 us (14%)
  matrix products  71.2 us (7%)
  local copies, waits for them, and re-layouts  22.9 us (2%)
  other arithmetic  21.1 us (2%)
  between operations  19.7 us (2%)
    reduce_scatter x1, waiting for transfers between devices, per_device(): lax.psum_scatter(g02, 'shard', scatter_dimension=0, tiled=True)  191 us
    reduce_scatter x1, waiting for transfers between devices, per_device(): lax.psum_scatter(g09, 'shard', scatter_dimension=0, tiled=True)  163 us
    reduce_scatter x1, waiting for transfers between devices, per_device(): lax.psum_scatter(g11, 'shard', scatter_dimension=0, tiled=True)  95.5 us
    unnamed x4, blocking collectives  92 us
    all_gather x1, waiting for transfers between devices, per_device(): lax.all_gather(up_weight, 'shard', axis=0, tiled=True)  78.2 us
    all_gather x1, waiting for transfers between devices, per_device(): lax.all_gather(down_weight, 'shard', axis=0, tiled=True)  76.2 us
    reduce_scatter x1, waiting for transfers between devices, per_device(): lax.psum_scatter(g05, 'shard', scatter_dimension=0, tiled=True)  41.4 us
    all_gather x1, blocking collectives, per_device(): lax.all_gather(up_bias, 'shard', axis=0, tiled=True)  26.5 us
  transfers between devices with their start and end apart: 13, of which 11 were waited for; matrix products, arithmetic and copies ran while one was open for 10% of the time, Pallas kernels for 0%

profile of v1, /device:TPU:0, one launch (start us, length us, event | category | flops | bytes accessed | tf_op | source)
XLA Modules:
  0.0 1018.3 jit_solution(12482183160917314412)
XLA Ops:
  18.7 40.4 %all-reduce.36 = (bf16[768]{0:T(1024)(128)(2,1)S(1)}, bf16[768]{0:T(1024)(128)(2,1)S(1)}, bf16[768]{0:T(1024)(128)(2,1)S(1)}, bf16[768]{0:T(1024)(128)(2,1)S(1)}...) all-reduce(bf16[768]{0:T(1024)(128)(2,1)S(1)} %dynamic-update-slice, ...), channel_id=1, replica_groups=mesh['rep'=4,'shard'=8] {'shard'}, use_global_device_ids=true, to_apply=%add.1 | all-reduce | flops 6144 | bytes 24576
  60.5 26.5 %all-gather = bf16[8,1,384]{2,1,0:T(2,128)(2,1)S(1)} all-gather(bf16[1,1,384]{2,1,0:T(2,128)(2,1)S(1)} %reshape.380), channel_id=1, replica_groups=mesh['rep'=4,'shard'=8] {'shard'}, dimensions={0}, use_global_device_ids=true | all-gather | bytes 6912 | tf_op jit(solution)/shard_map/all_gather | solution.py:247
  99.2 21.3 %all-gather.8.cloned.1.call-done = bf16[768,768]{1,0:T(8,128)(2,1)} async-done(((bf16[96,768]{1,0:T(8,128)(2,1)}), bf16[768,768]{1,0:T(8,128)(2,1)}) %all-gather.8.cloned.1.call-update) | async-done | bytes 1179664 | tf_op jit(solution)/shard_map/all_gather | solution.py:242
  122.5 78.2 %all-gather.10.cloned.1.call-done = bf16[768,3072]{1,0:T(8,128)(2,1)} async-done(((bf16[96,3072]{1,0:T(8,128)(2,1)}), bf16[768,3072]{1,0:T(8,128)(2,1)}) %all-gather.10.cloned.1.call-update) | async-done | bytes 4718608 | tf_op jit(solution)/shard_map/all_gather | solution.py:246
  204.3 76.2 %all-gather.12.cloned.1.call-done = bf16[3072,768]{1,0:T(8,128)(2,1)} async-done(((bf16[384,768]{1,0:T(8,128)(2,1)}), bf16[3072,768]{1,0:T(8,128)(2,1)}) %all-gather.12.cloned.1.call-update) | async-done | bytes 4718608 | tf_op jit(solution)/shard_map/all_gather | solution.py:269
  306.0 5.6 fusion.23
  311.6 5.5 fusion.109
  322.6 6.5 fusion.56
  329.2 5.6 fusion.80
  343.0 41.4 %reduce-scatter.13.cloned.1.call-done = f32[96,768]{1,0:T(8,128)} async-done(((f32[768,768]{1,0:T(8,128)}), f32[96,768]{1,0:T(8,128)}) %reduce-scatter.13.cloned.1.call-update) | async-done | bytes 294928 | tf_op jit(solution)/shard_map/reduce_scatter | solution.py:280
  386.1 191.1 %reduce-scatter.9.cloned.1.call-done = f32[96,2304]{1,0:T(8,128)} async-done(((f32[768,2304]{1,0:T(8,128)}), f32[96,2304]{1,0:T(8,128)}) %reduce-scatter.9.cloned.1.call-update) | async-done | bytes 884752 | tf_op jit(solution)/shard_map/reduce_scatter | solution.py:277
  579.2 162.8 %reduce-scatter.17.cloned.1.call-done = f32[96,3072]{1,0:T(8,128)} async-done(((f32[768,3072]{1,0:T(8,128)}), f32[96,3072]{1,0:T(8,128)}) %reduce-scatter.17.cloned.1.call-update) | async-done | bytes 1179664 | tf_op jit(solution)/shard_map/reduce_scatter | solution.py:284
  753.1 38.6 %all-reduce.35 = (bf16[768]{0:T(1024)(128)(2,1)S(1)}, bf16[768]{0:T(1024)(128)(2,1)S(1)}, bf16[768]{0:T(1024)(128)(2,1)S(1)}, bf16[768]{0:T(1024)(128)(2,1)S(1)}...) all-reduce(f32[768]{0:T(1024)S(1)} %get-tuple-element.17, ...), channel_id=2, replica_groups=mesh['rep'=4,'shard'=8] {'shard'}, use_global_device_ids=true, to_apply=%region_11.0.clone | all-reduce | flops 9216 | bytes 55296
  792.5 6.4 all-reduce.38
  801.4 6.6 all-reduce.37
  812.8 95.5 %reduce-scatter.21.cloned.1.call-done = f32[384,768]{1,0:T(8,128)} async-done(((f32[3072,768]{1,0:T(8,128)}), f32[384,768]{1,0:T(8,128)}) %reduce-scatter.21.cloned.1.call-update) | async-done | bytes 1179664 | tf_op jit(solution)/shard_map/reduce_scatter | solution.py:286
  917.0 13.1 %reduce-scatter.15.cloned.1.call-done = bf16[24,768]{1,0:T(8,128)(2,1)} async-done(((bf16[96,768]{1,0:T(8,128)(2,1)}), bf16[24,768]{1,0:T(8,128)(2,1)}) %reduce-scatter.15.cloned.1.call-update) | async-done | bytes 36880 | tf_op jit(solution)/shard_map/reduce_scatter | solution.py:306
  930.1 5.7 all_gather.101
  936.5 17.1 %reduce-scatter.11.cloned.1.call-done = bf16[24,2304]{1,0:T(8,128)(2,1)} async-done(((bf16[96,2304]{1,0:T(8,128)(2,1)}), bf16[24,2304]{1,0:T(8,128)(2,1)}) %reduce-scatter.11.cloned.1.call-update) | async-done | bytes 110608 | tf_op jit(solution)/shard_map/reduce_scatter | solution.py:297
  953.6 6.5 all_gather.98
  961.0 17.7 %reduce-scatter.19.cloned.1.call-done = bf16[24,3072]{1,0:T(8,128)(2,1)} async-done(((bf16[96,3072]{1,0:T(8,128)(2,1)}), bf16[24,3072]{1,0:T(8,128)(2,1)}) %reduce-scatter.19.cloned.1.call-update) | async-done | bytes 147472 | tf_op jit(solution)/shard_map/reduce_scatter | solution.py:318
  978.7 7.1 all_gather.105
  987.0 16.2 %reduce-scatter.23.cloned.1.call-done = bf16[96,768]{1,0:T(8,128)(2,1)} async-done(((bf16[384,768]{1,0:T(8,128)(2,1)}), bf16[96,768]{1,0:T(8,128)(2,1)}) %reduce-scatter.23.cloned.1.call-update) | async-done | bytes 147472 | tf_op jit(solution)/shard_map/reduce_scatter | solution.py:324
  1003.2 7.1 all_gather.107
  (166 shorter events, 100.0 us)
Async XLA Ops:
  7.2 80.9 %copy-start = (bf16[1,197,768]{2,1,0:T(8,128)(2,1)S(1)}, bf16[1,197,768]{2,1,0:T(8,128)(2,1)}, u32[]{:S(2)}) copy-start(bf16[1,197,768]{2,1,0:T(8,128)(2,1)} %param.16) | copy-start | bytes 907780
  7.2 81.2 %all-gather.6.cloned.1.call-start = ((), (), s32[]{:S(2)}) async-start(), calls=%async_computation.9 | async-start | bytes 3981312 | tf_op jit(solution)/shard_map/all_gather | solution.py:239
  7.9 112.5 %all-gather.8.cloned.1.call-start = ((), (), s32[]{:S(2)}) async-start(), calls=%async_computation.10 | async-start | bytes 1327104 | tf_op jit(solution)/shard_map/all_gather | solution.py:242
  8.7 192.0 %all-gather.10.cloned.1.call-start = ((), (), s32[]{:S(2)}) async-start(), calls=%async_computation.11 | async-start | bytes 5308416 | tf_op jit(solution)/shard_map/all_gather | solution.py:246
  9.4 271.1 %all-gather.12.cloned.1.call-start = ((), (), s32[]{:S(2)}) async-start(), calls=%async_computation.12 | async-start | bytes 5308416 | tf_op jit(solution)/shard_map/all_gather | solution.py:269
  10.0 374.4 %reduce-scatter.13.cloned.1.call-start = ((), (), s32[]{:S(2)}) async-start(), calls=%async_computation.15 | async-start | bytes 2654208 | tf_op jit(solution)/shard_map/reduce_scatter | solution.py:280
  95.2 1.7 copy-start.7
  96.9 23.6 %copy-start.4 = (f32[12,197,197]{1,2,0:T(8,128)}, f32[12,197,197]{1,2,0:T(8,128)S(1)}, u32[]{:S(2)}) copy-start(f32[12,197,197]{1,2,0:T(8,128)S(1)} %fusion.118) | copy-start | bytes 5588500
  99.2 101.5 %copy-start.5 = (bf16[12,64,197]{2,1,0:T(8,128)(2,1)}, bf16[12,64,197]{2,1,0:T(8,128)(2,1)S(1)}, u32[]{:S(2)}) copy-start(bf16[12,64,197]{2,1,0:T(8,128)(2,1)S(1)} %convolution_convert_fusion) | copy-start | bytes 907780
  280.5 4.4 copy-start.2
  284.8 1.8 copy-start.9
  284.8 2.0 copy-start.8
  286.7 1.4 copy-start.6
  287.2 0.8 copy-start.1
  289.9 287.3 %reduce-scatter.9.cloned.1.call-start = ((), (), s32[]{:S(2)}) async-start(), calls=%async_computation.13 | async-start | bytes 7962624 | tf_op jit(solution)/shard_map/reduce_scatter | solution.py:277
  322.6 419.5 %reduce-scatter.17.cloned.1.call-start = ((), (), s32[]{:S(2)}) async-start(), calls=%async_computation.17 | async-start | bytes 10616832 | tf_op jit(solution)/shard_map/reduce_scatter | solution.py:284
  329.2 579.0 %reduce-scatter.21.cloned.1.call-start = ((), (), s32[]{:S(2)}) async-start(), calls=%async_computation.19 | async-start | bytes 10616832 | tf_op jit(solution)/shard_map/reduce_scatter | solution.py:286
  338.3 574.3 %all-to-all-start = ((bf16[8,384,768]{2,1,0:T(8,128)(2,1)}), bf16[8,384,768]{2,1,0:T(8,128)(2,1)}, u32[]{:S(2)}, u32[]{:S(2)}) async-start(bf16[8,384,768]{2,1,0:T(8,128)(2,1)} %stack.2), calls=%async_computation | async-start | bytes 9437184 | tf_op jit(solution)/shard_map/all_to_all | solution.py:249
  343.0 587.1 %reduce-scatter.15.cloned.1.call-start = ((), (), s32[]{:S(2)}) async-start(), calls=%async_computation.16 | async-start | bytes 184320 | tf_op jit(solution)/shard_map/reduce_scatter | solution.py:306
  386.0 567.5 %reduce-scatter.11.cloned.1.call-start = ((), (), s32[]{:S(2)}) async-start(), calls=%async_computation.14 | async-start | bytes 552960 | tf_op jit(solution)/shard_map/reduce_scatter | solution.py:297
  579.2 399.6 %reduce-scatter.19.cloned.1.call-start = ((), (), s32[]{:S(2)}) async-start(), calls=%async_computation.18 | async-start | bytes 737280 | tf_op jit(solution)/shard_map/reduce_scatter | solution.py:318
  744.2 259.0 %reduce-scatter.23.cloned.1.call-start = ((), (), s32[]{:S(2)}) async-start(), calls=%async_computation.20 | async-start | bytes 737280 | tf_op jit(solution)/shard_map/reduce_scatter | solution.py:324
  752.2 0.8 copy-start.3
Sparse Core Ops, SparseCore 0:
  10.2 68.0 all-gather.5
  80.4 39.9 all-gather.7
  122.7 78.0 all-gather.9
  202.7 77.6 all-gather.11
  290.0 94.3 reduce-scatter.12
  387.9 189.2 reduce-scatter.8
  580.7 161.2 reduce-scatter.16
  745.6 162.5 reduce-scatter.20
  911.2 18.8 reduce-scatter.14
  932.4 21.0 reduce-scatter.10
  956.6 22.0 reduce-scatter.18
  981.1 22.0 reduce-scatter.22
